TPU v7x, 32 devices: a whole 2x2x4 slice. The times are simulated.
32 devices in a mesh: dp: 8 (over y, x, core), fsdp: 4 (over z).
Axes of the slice: x: 2, y: 2, z: 4, core: 2. Of those that a mesh axis runs over, the one named last changes fastest.
Arguments:
- tokens: bfloat16 [32, 256, 1152], P(('dp', 'fsdp')), may hold values from -6 to 6
- condition: bfloat16 [32, 1152], P(('dp', 'fsdp')), may hold values from -6 to 6
- grid_sizes: int32 [32, 2], P(('dp', 'fsdp')), may hold values from 12 to 20, as said below
- w_ada: bfloat16 [1152, 6912], P('fsdp'), may hold values from -0.1875 to 0.1875
- w_qkv: bfloat16 [1152, 3456], P('fsdp'), may hold values from -0.1875 to 0.1875
- w_out: bfloat16 [1152, 1152], P('fsdp'), may hold values from -1 to 1
- w_up: bfloat16 [1152, 4608], P('fsdp'), may hold values from -0.1875 to 0.1875
- w_down: bfloat16 [4608, 1152], P('fsdp'), may hold values from -0.09375 to 0.09375
- b_ada: bfloat16 [6912], P('fsdp'), may hold values from -3 to 3
- b_qv: bfloat16 [2304], P('fsdp'), may hold values from -3 to 3
- b_out: bfloat16 [1152], P('fsdp'), may hold values from -3 to 3
- b_up: bfloat16 [4608], P('fsdp'), may hold values from -3 to 3
- b_down: bfloat16 [1152], P('fsdp'), may hold values from -3 to 3
- cotangent: bfloat16 [32, 256, 1152], P(('dp', 'fsdp')), may hold values from -6 to 6
Outputs:
- output: bfloat16 [32, 256, 1152], P(('dp', 'fsdp'))
- grad_tokens: bfloat16 [32, 256, 1152], P(('dp', 'fsdp'))
- grad_condition: float32 [32, 1152], P(('dp', 'fsdp'))
- grad_w_ada: float32 [1152, 6912], P('fsdp', 'dp')
- grad_w_qkv: float32 [1152, 3456], P('fsdp', 'dp')
- grad_w_out: float32 [1152, 1152], P('fsdp', 'dp')
- grad_w_up: float32 [1152, 4608], P('fsdp', 'dp')
- grad_w_down: float32 [4608, 1152], P('fsdp', 'dp')
- grad_b_ada: float32 [6912], P('fsdp')
- grad_b_qv: float32 [2304], P('fsdp')
- grad_b_out: float32 [1152], P('fsdp')
- grad_b_up: float32 [4608], P('fsdp')
- grad_b_down: float32 [1152], P('fsdp')
Inputs may be any that keep to these rules, and one draw needn't show every extreme that they name: `grid_sizes`: each image grid has 12 to 20 rows and columns and at most 256 tokens; image 0 has 12 rows and 20 columns, and image 1 has 20 rows and 12 columns.
All inputs are finite; a program needn't handle non-finite values.
Results may differ from a plain program's by a relative error of at most 0.015.
The roundings to bfloat16 on the way count: a program that leaves them out, or rounds other values in their place, can miss the bound.
Values may be sent and summed in bfloat16 or wider, within the bound.
No kernel may reach another device: no remote copies, remote signals or barrier semaphores. Data moves between devices by JAX's collectives and lax.ppermute only.
A program may use at most 256 MiB of HBM per device.

v0:
```python
import math
import jax
import jax.numpy as jnp
from jax import lax
from jax.sharding import PartitionSpec as P

HEAD_DIM = 72
epsilon = 1e-06
masked_value = -1e30
gelu_root = math.sqrt(2.0 / math.pi)


def layer_norm(values_in):
    centred = values_in - jnp.mean(values_in, axis=-1, keepdims=True)
    spread = jnp.mean(centred * centred, axis=-1, keepdims=True)
    return centred * lax.rsqrt(spread + epsilon)


def gelu_tanh(pre_act):
    return (
        0.5
        * pre_act
        * (1.0 + jnp.tanh(gelu_root * (pre_act + 0.044715 * pre_act * pre_act * pre_act)))
    )


def apply_rows(left, right):
    return jnp.einsum("isd,de->ise", left, right, preferred_element_type=jnp.float32)


def forward_pass(weights_full, tokens_wide, cond_act, live_keys, kept_lse):
    w_ada, w_qkv, w_out, w_up, w_down, b_ada, b_qv, b_out, b_up, b_down = weights_full
    width = w_out.shape[0]
    images = tokens_wide.shape[0]
    slots = tokens_wide.shape[1]
    heads = width // HEAD_DIM
    modulation = jnp.dot(cond_act, w_ada, preferred_element_type=jnp.float32) + b_ada.astype(
        jnp.float32
    )
    portions = jnp.split(modulation, 6, axis=1)
    modulated = tuple((portion[:, None, :] for portion in portions))
    shift_one, scale_one, gate_one, shift_two, scale_two, gate_two = modulated
    norm_one = layer_norm(tokens_wide)
    normed = (norm_one * (1.0 + scale_one) + shift_one).astype(jnp.bfloat16)
    projected = apply_rows(normed, w_qkv)
    bias_qv = b_qv.astype(jnp.float32)
    queries = (
        (projected[..., :width] + bias_qv[:width])
        .astype(jnp.bfloat16)
        .reshape(images, slots, heads, HEAD_DIM)
    )
    key_part = (
        projected[..., width : 2 * width]
        .astype(jnp.bfloat16)
        .reshape(images, slots, heads, HEAD_DIM)
    )
    values = (
        (projected[..., 2 * width :] + bias_qv[width:])
        .astype(jnp.bfloat16)
        .reshape(images, slots, heads, HEAD_DIM)
    )
    raw = jnp.einsum(
        "iqhe,ikhe->ihqk", queries, key_part, preferred_element_type=jnp.float32
    ) * HEAD_DIM ** (-0.5)
    scores = jnp.where(live_keys[:, None, None, :], raw, masked_value)
    if kept_lse is None:
        highest = jnp.max(scores, axis=-1, keepdims=True)
        lse = highest + jnp.log(jnp.sum(jnp.exp(scores - highest), axis=-1, keepdims=True))
    else:
        lse = kept_lse
    probs = jnp.exp(scores - lse)
    probs_low = probs.astype(jnp.bfloat16)
    attended = jnp.einsum("ihqk,ikhe->iqhe", probs_low, values, preferred_element_type=jnp.float32)
    attended = attended.reshape(images, slots, width).astype(jnp.bfloat16)
    attn_out = apply_rows(attended, w_out) + b_out.astype(jnp.float32)
    middle = tokens_wide + gate_one * attn_out
    norm_two = layer_norm(middle)
    normed_two = (norm_two * (1.0 + scale_two) + shift_two).astype(jnp.bfloat16)
    pre_act = apply_rows(normed_two, w_up) + b_up.astype(jnp.float32)
    activated = gelu_tanh(pre_act).astype(jnp.bfloat16)
    mlp_out = apply_rows(activated, w_down) + b_down.astype(jnp.float32)
    return (
        modulated,
        norm_one,
        normed,
        queries,
        key_part,
        values,
        lse,
        probs,
        probs_low,
        attended,
        attn_out,
        middle,
        norm_two,
        normed_two,
        pre_act,
        activated,
        mlp_out,
    )


def body(
    tokens,
    condition,
    grid_sizes,
    w_ada,
    w_qkv,
    w_out,
    w_up,
    w_down,
    b_ada,
    b_qv,
    b_out,
    b_up,
    b_down,
    cotangent,
):
    weights_full = (
        lax.all_gather(w_ada, "fsdp", axis=0, tiled=True),
        lax.all_gather(w_qkv, "fsdp", axis=0, tiled=True),
        lax.all_gather(w_out, "fsdp", axis=0, tiled=True),
        lax.all_gather(w_up, "fsdp", axis=0, tiled=True),
        lax.all_gather(w_down, "fsdp", axis=0, tiled=True),
        lax.all_gather(b_ada, "fsdp", axis=0, tiled=True),
        lax.all_gather(b_qv, "fsdp", axis=0, tiled=True),
        lax.all_gather(b_out, "fsdp", axis=0, tiled=True),
        lax.all_gather(b_up, "fsdp", axis=0, tiled=True),
        lax.all_gather(b_down, "fsdp", axis=0, tiled=True),
    )
    images = tokens.shape[0]
    slots = tokens.shape[1]
    width = tokens.shape[2]
    heads = width // HEAD_DIM
    live_counts = grid_sizes[:, 0] * grid_sizes[:, 1]
    live_keys = lax.broadcasted_iota(jnp.int32, (images, slots), 1) < live_counts[:, None]
    live_rows = live_keys.astype(jnp.float32)[:, :, None]
    tokens_wide = tokens.astype(jnp.float32)
    cond_wide = condition.astype(jnp.float32)
    cond_act = (cond_wide * jax.nn.sigmoid(cond_wide)).astype(jnp.bfloat16)
    saved = forward_pass(weights_full, tokens_wide, cond_act, live_keys, None)
    middle_first = saved[11]
    gate_first = saved[0][5]
    mlp_first = saved[16]
    output = (live_rows * (middle_first + gate_first * mlp_first)).astype(jnp.bfloat16)
    weights_back = (
        lax.all_gather(w_ada, "fsdp", axis=0, tiled=True),
        lax.all_gather(w_qkv, "fsdp", axis=0, tiled=True),
        lax.all_gather(w_out, "fsdp", axis=0, tiled=True),
        lax.all_gather(w_up, "fsdp", axis=0, tiled=True),
        lax.all_gather(w_down, "fsdp", axis=0, tiled=True),
        lax.all_gather(b_ada, "fsdp", axis=0, tiled=True),
        lax.all_gather(b_qv, "fsdp", axis=0, tiled=True),
        lax.all_gather(b_out, "fsdp", axis=0, tiled=True),
        lax.all_gather(b_up, "fsdp", axis=0, tiled=True),
        lax.all_gather(b_down, "fsdp", axis=0, tiled=True),
    )
    saved = forward_pass(weights_back, tokens_wide, cond_act, live_keys, saved[6])
    (
        modulated,
        norm_one,
        normed,
        queries,
        key_part,
        values,
        lse,
        probs,
        probs_low,
        attended,
        attn_out,
        middle,
        norm_two,
        normed_two,
        pre_act,
        activated,
        mlp_out,
    ) = saved
    shift_one, scale_one, gate_one, shift_two, scale_two, gate_two = modulated
    ada_full, qkv_full, out_full, up_full, down_full = (
        weights_back[0],
        weights_back[1],
        weights_back[2],
        weights_back[3],
        weights_back[4],
    )
    upstream = live_rows * cotangent.astype(jnp.float32)
    d_gate_two = jnp.sum(upstream * mlp_out, axis=1)
    d_mlp = (gate_two * upstream).astype(jnp.bfloat16)
    grad_w_down = jnp.einsum("isf,isd->fd", activated, d_mlp, preferred_element_type=jnp.float32)
    grad_b_down = jnp.sum(d_mlp.astype(jnp.float32), axis=(0, 1))
    d_act = jnp.einsum("isd,fd->isf", d_mlp, down_full, preferred_element_type=jnp.float32)
    unused_gelu, gelu_pull = jax.vjp(gelu_tanh, pre_act)
    d_pre = gelu_pull(d_act)[0].astype(jnp.bfloat16)
    grad_w_up = jnp.einsum("isd,isf->df", normed_two, d_pre, preferred_element_type=jnp.float32)
    grad_b_up = jnp.sum(d_pre.astype(jnp.float32), axis=(0, 1))
    d_normed_two = jnp.einsum("isf,df->isd", d_pre, up_full, preferred_element_type=jnp.float32)
    d_shift_two = jnp.sum(d_normed_two, axis=1)
    d_scale_two = jnp.sum(d_normed_two * norm_two, axis=1)
    unused_norm, second_pull = jax.vjp(layer_norm, middle)
    d_middle = upstream + second_pull(d_normed_two * (1.0 + scale_two))[0]
    d_gate_one = jnp.sum(d_middle * attn_out, axis=1)
    d_attn = (gate_one * d_middle).astype(jnp.bfloat16)
    grad_w_out = jnp.einsum("isd,ise->de", attended, d_attn, preferred_element_type=jnp.float32)
    grad_b_out = jnp.sum(d_attn.astype(jnp.float32), axis=(0, 1))
    d_attended = jnp.einsum("ise,de->isd", d_attn, out_full, preferred_element_type=jnp.float32)
    d_attended = d_attended.astype(jnp.bfloat16).reshape(images, slots, heads, HEAD_DIM)
    d_probs = jnp.einsum("iqhe,ikhe->ihqk", d_attended, values, preferred_element_type=jnp.float32)
    d_values = jnp.einsum(
        "ihqk,iqhe->ikhe", probs_low, d_attended, preferred_element_type=jnp.float32
    ).astype(jnp.bfloat16)
    row_inner = jnp.sum(probs * d_probs, axis=-1, keepdims=True)
    d_scores = (probs * (d_probs - row_inner)).astype(jnp.bfloat16)
    d_queries = (
        jnp.einsum("ihqk,ikhe->iqhe", d_scores, key_part, preferred_element_type=jnp.float32)
        * HEAD_DIM ** (-0.5)
    ).astype(jnp.bfloat16)
    d_keys = (
        jnp.einsum("ihqk,iqhe->ikhe", d_scores, queries, preferred_element_type=jnp.float32)
        * HEAD_DIM ** (-0.5)
    ).astype(jnp.bfloat16)
    d_projected = jnp.concatenate(
        [
            d_queries.reshape(images, slots, width),
            d_keys.reshape(images, slots, width),
            d_values.reshape(images, slots, width),
        ],
        axis=2,
    )
    grad_w_qkv = jnp.einsum("isd,ise->de", normed, d_projected, preferred_element_type=jnp.float32)
    grad_b_qv = jnp.concatenate(
        [
            jnp.sum(d_queries.astype(jnp.float32), axis=(0, 1)).reshape(width),
            jnp.sum(d_values.astype(jnp.float32), axis=(0, 1)).reshape(width),
        ]
    )
    d_normed = jnp.einsum("ise,de->isd", d_projected, qkv_full, preferred_element_type=jnp.float32)
    d_shift_one = jnp.sum(d_normed, axis=1)
    d_scale_one = jnp.sum(d_normed * norm_one, axis=1)
    unused_first, first_pull = jax.vjp(layer_norm, tokens_wide)
    grad_tokens = (d_middle + first_pull(d_normed * (1.0 + scale_one))[0]).astype(jnp.bfloat16)
    d_modulation = jnp.concatenate(
        [d_shift_one, d_scale_one, d_gate_one, d_shift_two, d_scale_two, d_gate_two], axis=1
    ).astype(jnp.bfloat16)
    grad_w_ada = jnp.einsum("id,ie->de", cond_act, d_modulation, preferred_element_type=jnp.float32)
    grad_b_ada = jnp.sum(d_modulation.astype(jnp.float32), axis=0)
    d_cond_act = jnp.einsum("ie,de->id", d_modulation, ada_full, preferred_element_type=jnp.float32)
    unused_silu, silu_pull = jax.vjp(lambda inner: inner * jax.nn.sigmoid(inner), cond_wide)
    grad_condition = silu_pull(d_cond_act)[0]
    narrow = (
        lax.psum_scatter(
            grad_w_ada.astype(jnp.bfloat16), "fsdp", scatter_dimension=0, tiled=True
        ).astype(jnp.float32),
        lax.psum_scatter(
            grad_w_qkv.astype(jnp.bfloat16), "fsdp", scatter_dimension=0, tiled=True
        ).astype(jnp.float32),
        lax.psum_scatter(
            grad_w_out.astype(jnp.bfloat16), "fsdp", scatter_dimension=0, tiled=True
        ).astype(jnp.float32),
        lax.psum_scatter(
            grad_w_up.astype(jnp.bfloat16), "fsdp", scatter_dimension=0, tiled=True
        ).astype(jnp.float32),
        lax.psum_scatter(
            grad_w_down.astype(jnp.bfloat16), "fsdp", scatter_dimension=0, tiled=True
        ).astype(jnp.float32),
        lax.psum_scatter(
            grad_b_ada.astype(jnp.bfloat16), "fsdp", scatter_dimension=0, tiled=True
        ).astype(jnp.float32),
        lax.psum_scatter(
            grad_b_qv.astype(jnp.bfloat16), "fsdp", scatter_dimension=0, tiled=True
        ).astype(jnp.float32),
        lax.psum_scatter(
            grad_b_out.astype(jnp.bfloat16), "fsdp", scatter_dimension=0, tiled=True
        ).astype(jnp.float32),
        lax.psum_scatter(
            grad_b_up.astype(jnp.bfloat16), "fsdp", scatter_dimension=0, tiled=True
        ).astype(jnp.float32),
        lax.psum_scatter(
            grad_b_down.astype(jnp.bfloat16), "fsdp", scatter_dimension=0, tiled=True
        ).astype(jnp.float32),
    )
    summed_weights = (
        lax.psum_scatter(narrow[0], "dp", scatter_dimension=1, tiled=True),
        lax.psum_scatter(narrow[1], "dp", scatter_dimension=1, tiled=True),
        lax.psum_scatter(narrow[2], "dp", scatter_dimension=1, tiled=True),
        lax.psum_scatter(narrow[3], "dp", scatter_dimension=1, tiled=True),
        lax.psum_scatter(narrow[4], "dp", scatter_dimension=1, tiled=True),
    )
    summed_biases = lax.psum((narrow[5], narrow[6], narrow[7], narrow[8], narrow[9]), "dp")
    return (
        output,
        grad_tokens,
        grad_condition,
        summed_weights[0],
        summed_weights[1],
        summed_weights[2],
        summed_weights[3],
        summed_weights[4],
        summed_biases[0],
        summed_biases[1],
        summed_biases[2],
        summed_biases[3],
        summed_biases[4],
    )


def solution(mesh):
    return jax.shard_map(
        body,
        mesh=mesh,
        in_specs=(
            P(("dp", "fsdp"), None, None),
            P(("dp", "fsdp"), None),
            P(("dp", "fsdp"), None),
            P("fsdp", None),
            P("fsdp", None),
            P("fsdp", None),
            P("fsdp", None),
            P("fsdp", None),
            P("fsdp"),
            P("fsdp"),
            P("fsdp"),
            P("fsdp"),
            P("fsdp"),
            P(("dp", "fsdp"), None, None),
        ),
        out_specs=(
            P(("dp", "fsdp"), None, None),
            P(("dp", "fsdp"), None, None),
            P(("dp", "fsdp"), None),
            P("fsdp", "dp"),
            P("fsdp", "dp"),
            P("fsdp", "dp"),
            P("fsdp", "dp"),
            P("fsdp", "dp"),
            P("fsdp"),
            P("fsdp"),
            P("fsdp"),
            P("fsdp"),
            P("fsdp"),
        ),
        check_vma=False,
    )
```

profile of v0, /device:TPU:0, one launch (start us, length us, event | category | flops | bytes accessed | tf_op | source)
XLA Modules:
  0.0 2053.4 jit_solution(9514321274415671537)
XLA Ops:
  14.4 21.8 %all-reduce.11 = (bf16[2304]{0:T(1024)(128)(2,1)S(1)}, bf16[6912]{0:T(1024)(128)(2,1)S(1)}, bf16[1152]{0:T(1024)(128)(2,1)S(1)}, bf16[1152]{0:T(1024)(128)(2,1)}) all-reduce(bf16[2304]{0:T(1024)(128)(2,1)S(1)} %dynamic-update-slice.1, bf16[6912]{0:T(1024)(128)(2,1)S(1)} %dynamic-update-slice, ...), channel_id=1, replica_groups=mesh['dp'=8,'fsdp'=4] {'fsdp'}, use_global_device_ids=true, to_apply=%add.1 | all-reduce | flops 11520 | bytes 46080
  36.8 17.0 all-gather
  58.1 227.6 %all-gather.7.cloned.1.call-done = bf16[1152,6912]{1,0:T(8,128)(2,1)} async-done(((bf16[288,6912]{1,0:T(8,128)(2,1)}), bf16[1152,6912]{1,0:T(8,128)(2,1)}) %all-gather.7.cloned.1.call-update) | async-done | bytes 15925264 | tf_op jit(solution)/shard_map/all_gather | solution.py:120
  285.7 7.7 convolution_reduce_fusion
  294.2 134.1 %all-gather.9.cloned.1.call-done = bf16[1152,3456]{1,0:T(8,128)(2,1)} async-done(((bf16[288,3456]{1,0:T(8,128)(2,1)}), bf16[1152,3456]{1,0:T(8,128)(2,1)}) %all-gather.9.cloned.1.call-update) | async-done | bytes 7962640 | tf_op jit(solution)/shard_map/all_gather | solution.py:121
  428.3 6.0 convolution_bitcast_fusion
  434.3 0.9 slice.46
  435.8 1.3 copy.53
  437.1 1.1 fusion.6
  438.3 1.0 exponential_reduce_fusion
  439.3 0.9 copy-done
  440.2 1.7 convolution_convert_fusion.6
  441.9 41.5 %all-gather.11.cloned.1.call-done = bf16[1152,1152]{1,0:T(8,128)(2,1)} async-done(((bf16[288,1152]{1,0:T(8,128)(2,1)}), bf16[1152,1152]{1,0:T(8,128)(2,1)}) %all-gather.11.cloned.1.call-update) | async-done | bytes 2654224 | tf_op jit(solution)/shard_map/all_gather | solution.py:122
  483.4 3.9 fusion.60
  489.3 180.4 %all-gather.13.cloned.1.call-done = bf16[1152,4608]{1,0:T(8,128)(2,1)} async-done(((bf16[288,4608]{1,0:T(8,128)(2,1)}), bf16[1152,4608]{1,0:T(8,128)(2,1)}) %all-gather.13.cloned.1.call-update) | async-done | bytes 10616848 | tf_op jit(solution)/shard_map/all_gather | solution.py:123
  669.7 9.3 convolution_add_fusion
  679.0 176.4 %all-gather.15.cloned.1.call-done = bf16[4608,1152]{1,0:T(8,128)(2,1)} async-done(((bf16[1152,1152]{1,0:T(8,128)(2,1)}), bf16[4608,1152]{1,0:T(8,128)(2,1)}) %all-gather.15.cloned.1.call-update) | async-done | bytes 10616848 | tf_op jit(solution)/shard_map/all_gather | solution.py:124
  855.4 10.1 fusion.64
  865.5 8.8 fusion.24
  874.8 1.0 copy-done.15
  875.8 1.0 fusion.58
  877.7 1.9 convolution_convert_fusion.4
  879.5 2.1 copy.55
  881.7 4.3 bitcast_reduce_fusion
  886.0 1.5 multiply_reduce_fusion
  887.5 1.4 multiply_convert_fusion.2
  889.7 1.2 bitcast_reduce_fusion.1
  891.7 5.8 convolution_convert_fusion.2
  898.2 8.7 convolution_convert_fusion.1
  907.0 1.4 convert_element_type.228
  908.4 1.3 convert.45
  910.3 7.0 fusion.20
  918.0 0.9 dynamic-update-slice.4
  919.6 1.9 fusion.18
  921.5 0.9 dynamic-update-slice.5
  923.1 11.8 fusion.23
  934.8 0.9 dynamic-update-slice.6
  935.7 0.9 dynamic-update-slice.7
  936.6 0.9 dynamic-update-slice.8
  937.4 0.9 dynamic-update-slice.9
  938.3 6.6 multiply_convert_fusion
  946.0 2.4 convolution_convert_fusion.3
  948.5 1.0 copy-done.16
  949.4 10.6 convolution_convert_fusion
  960.1 73.8 %reduce-scatter.23.cloned.1.call-done = bf16[288,3456]{1,0:T(8,128)(2,1)} async-done(((bf16[1152,3456]{1,0:T(8,128)(2,1)}), bf16[288,3456]{1,0:T(8,128)(2,1)}) %reduce-scatter.23.cloned.1.call-update) | async-done | bytes 1990672 | tf_op jit(solution)/shard_map/reduce_scatter | solution.py:253
  1034.0 4.5 copy.67
  1038.5 178.7 %reduce-scatter.27.cloned.1.call-done = bf16[288,4608]{1,0:T(8,128)(2,1)} async-done(((bf16[1152,4608]{1,0:T(8,128)(2,1)}), bf16[288,4608]{1,0:T(8,128)(2,1)}) %reduce-scatter.27.cloned.1.call-update) | async-done | bytes 2654224 | tf_op jit(solution)/shard_map/reduce_scatter | solution.py:259
  1217.2 5.5 copy.71
  1222.8 265.3 %reduce-scatter.21.cloned.1.call-done = bf16[288,6912]{1,0:T(8,128)(2,1)} async-done(((bf16[1152,6912]{1,0:T(8,128)(2,1)}), bf16[288,6912]{1,0:T(8,128)(2,1)}) %reduce-scatter.21.cloned.1.call-update) | async-done | bytes 3981328 | tf_op jit(solution)/shard_map/reduce_scatter | solution.py:250
  1488.1 7.7 copy.65
  1495.8 47.9 %reduce-scatter.25.cloned.1.call-done = bf16[288,1152]{1,0:T(8,128)(2,1)} async-done(((bf16[1152,1152]{1,0:T(8,128)(2,1)}), bf16[288,1152]{1,0:T(8,128)(2,1)}) %reduce-scatter.25.cloned.1.call-update) | async-done | bytes 663568 | tf_op jit(solution)/shard_map/reduce_scatter | solution.py:256
  1543.7 2.6 copy.69
  1546.4 179.5 %reduce-scatter.29.cloned.1.call-done = bf16[1152,1152]{1,0:T(8,128)(2,1)} async-done(((bf16[4608,1152]{1,0:T(8,128)(2,1)}), bf16[1152,1152]{1,0:T(8,128)(2,1)}) %reduce-scatter.29.cloned.1.call-update) | async-done | bytes 2654224 | tf_op jit(solution)/shard_map/reduce_scatter | solution.py:262
  1725.9 5.4 copy.73
  1734.2 19.1 all-reduce.10
  1753.7 23.5 %all-reduce.9 = (f32[1728]{0:T(1024)}, f32[576]{0:T(1024)}, f32[288]{0:T(512)}, f32[1152]{0:T(1024)}, f32[288]{0:T(512)}) all-reduce(f32[1728]{0:T(1024)S(1)} %dynamic-slice_convert_fusion.1, f32[576]{0:T(1024)S(1)} %dynamic-slice_convert_fusion.2, f32[288]{0:T(512)S(1)} %get-tuple-element.112, ...), channel_id=1, replica_groups=mesh['dp'=8,'fsdp'=4] {'dp'}, use_global_device_ids=true, to_apply=%region_28.29 | all-reduce | flops 4032 | bytes 32256 | tf_op jit(solution)/shard_map/psum | solution.py:288
  1777.1 10.4 fusion.40
  1787.7 2.1 copy.68
  1789.8 67.2 %reduce-scatter.37.cloned.1.call-done = f32[576,288]{1,0:T(8,128)} async-done(((f32[4608,288]{1,0:T(8,128)}), f32[576,288]{1,0:T(8,128)}) %reduce-scatter.37.cloned.1.call-update) | async-done | bytes 663568
  1857.0 2.3 copy.72
  1859.3 83.4 %reduce-scatter.31.cloned.1.call-done = f32[864,288]{1,0:T(8,128)} async-done(((f32[6912,288]{1,0:T(8,128)}), f32[864,288]{1,0:T(8,128)}) %reduce-scatter.31.cloned.1.call-update) | async-done | bytes 995344
  1942.7 2.7 copy.66
  1945.4 40.5 %reduce-scatter.35.cloned.1.call-done = f32[144,288]{1,0:T(8,128)} async-done(((f32[1152,288]{1,0:T(8,128)}), f32[144,288]{1,0:T(8,128)}) %reduce-scatter.35.cloned.1.call-update) | async-done | bytes 165904
  1985.9 60.8 %reduce-scatter.39.cloned.1.call-done = f32[144,1152]{1,0:T(8,128)} async-done(((f32[1152,1152]{1,0:T(8,128)}), f32[144,1152]{1,0:T(8,128)}) %reduce-scatter.39.cloned.1.call-update) | async-done | bytes 663568
  (202 shorter events, 20.5 us)
Async XLA Ops:
  7.2 278.5 %all-gather.7.cloned.1.call-start = ((), (), s32[]{:S(2)}) async-start(), calls=%async_computation.10 | async-start | bytes 19906560 | tf_op jit(solution)/shard_map/all_gather | solution.py:120
  7.9 420.3 %all-gather.9.cloned.1.call-start = ((), (), s32[]{:S(2)}) async-start(), calls=%async_computation.11 | async-start | bytes 9953280 | tf_op jit(solution)/shard_map/all_gather | solution.py:121
  8.7 474.8 %all-gather.11.cloned.1.call-start = ((), (), s32[]{:S(2)}) async-start(), calls=%async_computation.12 | async-start | bytes 3317760 | tf_op jit(solution)/shard_map/all_gather | solution.py:122
  9.4 1.3 copy-start.54
  9.4 3.9 copy-start.59
  9.4 4.1 copy-start.60
  9.4 4.4 copy-start.55
  9.4 4.6 copy-start.51
  9.5 27.4 %copy-start.52 = (bf16[1152]{0:T(1024)(128)(2,1)S(1)}, bf16[1152]{0:T(1024)(128)(2,1)}, u32[]{:S(2)}) copy-start(bf16[1152]{0:T(1024)(128)(2,1)} %param.25) | copy-start | bytes 6916
  9.5 45.0 %copy-start.56 = (s32[1,2]{1,0:T(1,128)S(1)}, s32[1,2]{1,0:T(1,128)}, u32[]{:S(2)}) copy-start(s32[1,2]{1,0:T(1,128)} %param.16) | copy-start | bytes 28
  9.5 47.5 %copy-start.2 = (bf16[1,256,1152]{2,1,0:T(8,128)(2,1)S(1)}, bf16[1,256,1152]{2,1,0:T(8,128)(2,1)}, u32[]{:S(2)}) copy-start(bf16[1,256,1152]{2,1,0:T(8,128)(2,1)} %param.14) | copy-start | bytes 1769476
  9.5 660.2 %all-gather.13.cloned.1.call-start = ((), (), s32[]{:S(2)}) async-start(), calls=%async_computation.13 | async-start | bytes 13271040 | tf_op jit(solution)/shard_map/all_gather | solution.py:123
  10.1 47.4 %copy-start.21 = (bf16[1,1152]{1,0:T(2,128)(2,1)S(1)}, bf16[1,1152]{1,0:T(2,128)(2,1)}, u32[]{:S(2)}) copy-start(bf16[1,1152]{1,0:T(2,128)(2,1)} %param.15) | copy-start | bytes 6916
  10.1 845.4 %all-gather.15.cloned.1.call-start = ((), (), s32[]{:S(2)}) async-start(), calls=%async_computation.14 | async-start | bytes 13271040 | tf_op jit(solution)/shard_map/all_gather | solution.py:124
  10.7 1023.3 %reduce-scatter.23.cloned.1.call-start = ((), (), s32[]{:S(2)}) async-start(), calls=%async_computation.16 | async-start | bytes 9953280 | tf_op jit(solution)/shard_map/reduce_scatter | solution.py:253
  56.4 381.9 %copy-start.47 = (pred[256]{0:T(512)(128)(4,1)}, pred[256]{0:T(512)(128)(4,1)S(1)}, u32[]{:S(2)}) copy-start(pred[256]{0:T(512)(128)(4,1)S(1)} %iota_compare_fusion) | copy-start | bytes 772
  57.1 371.1 %copy-start.38 = (f32[256]{0:T(256)}, f32[256]{0:T(256)S(1)}, u32[]{:S(2)}) copy-start(f32[256]{0:T(256)S(1)} %broadcast_multiply_fusion.1) | copy-start | bytes 3076
  57.4 236.0 %copy-start.42 = (f32[256]{0:T(256)}, f32[256]{0:T(256)S(1)}, u32[]{:S(2)}) copy-start(f32[256]{0:T(256)S(1)} %fusion.19) | copy-start | bytes 3076
  57.5 370.8 %copy-start.40 = (f32[256]{0:T(256)}, f32[256]{0:T(256)S(1)}, u32[]{:S(2)}) copy-start(f32[256]{0:T(256)S(1)} %fusion.45) | copy-start | bytes 3076
  58.1 235.3 %copy-start.23 = (f32[1,1152]{1,0:T(1,128)}, f32[1,1152]{1,0:T(1,128)S(1)}, u32[]{:S(2)}) copy-start(f32[1,1152]{1,0:T(1,128)S(1)} %get-tuple-element.81) | copy-start | bytes 13828
  294.2 140.1 %copy-start.27 = (f32[1152]{0:T(1024)}, f32[1152]{0:T(1024)S(1)}, u32[]{:S(2)}) copy-start(f32[1152]{0:T(1024)S(1)} %get-tuple-element.62) | copy-start | bytes 13828
  294.2 140.1 %copy-start.45 = (f32[1152]{0:T(1024)}, f32[1152]{0:T(1024)S(1)}, u32[]{:S(2)}) copy-start(f32[1152]{0:T(1024)S(1)} %get-tuple-element.61) | copy-start | bytes 13828
  435.6 3.7 copy-start.7
  438.3 2.0 copy-start
  855.4 10.1 copy-start.17
  855.4 10.1 copy-start.30
  855.4 10.1 copy-start.35
  865.5 8.8 copy-start.12
  865.5 8.9 copy-start.44
  874.3 2.5 copy-start.3
  874.3 1.5 copy-start.15
  874.3 1.5 copy-start.19
  874.3 1.5 copy-start.25
  874.4 1.5 copy-start.57
  874.4 3.3 copy-start.6
  874.8 2.1 copy-start.5
  874.8 2.0 copy-start.50
  881.7 4.3 copy-start.1
  881.7 4.3 copy-start.8
  881.7 4.3 copy-start.9
  881.7 4.3 copy-start.48
  886.0 4.9 copy-start.61
  889.6 2.1 copy-start.28
  889.6 2.1 copy-start.39
  889.6 2.1 copy-start.41
  889.7 2.1 copy-start.46
  897.6 319.6 %reduce-scatter.27.cloned.1.call-start = ((), (), s32[]{:S(2)}) async-start(), calls=%async_computation.18 | async-start | bytes 13271040 | tf_op jit(solution)/shard_map/reduce_scatter | solution.py:259
  906.9 2.7 copy-start.4
  907.0 581.1 %reduce-scatter.21.cloned.1.call-start = ((), (), s32[]{:S(2)}) async-start(), calls=%async_computation.15 | async-start | bytes 19906560 | tf_op jit(solution)/shard_map/reduce_scatter | solution.py:250
  919.6 1.9 copy-start.49
  944.9 598.8 %reduce-scatter.25.cloned.1.call-start = ((), (), s32[]{:S(2)}) async-start(), calls=%async_computation.17 | async-start | bytes 3317760 | tf_op jit(solution)/shard_map/reduce_scatter | solution.py:256
  948.4 777.5 %reduce-scatter.29.cloned.1.call-start = ((), (), s32[]{:S(2)}) async-start(), calls=%async_computation.19 | async-start | bytes 13271040 | tf_op jit(solution)/shard_map/reduce_scatter | solution.py:262
  960.1 827.6 %reduce-scatter.33.cloned.1.call-start = ((), (), s32[]{:S(2)}) async-start(), calls=%async_computation.21 | async-start | bytes 5971968
  1038.5 818.5 %reduce-scatter.37.cloned.1.call-start = ((), (), s32[]{:S(2)}) async-start(), calls=%async_computation.23 | async-start | bytes 7962624
  1222.7 720.0 %reduce-scatter.31.cloned.1.call-start = ((), (), s32[]{:S(2)}) async-start(), calls=%async_computation.20 | async-start | bytes 11943936
  1495.8 490.2 %reduce-scatter.35.cloned.1.call-start = ((), (), s32[]{:S(2)}) async-start(), calls=%async_computation.22 | async-start | bytes 1990656
  1546.4 500.3 %reduce-scatter.39.cloned.1.call-start = ((), (), s32[]{:S(2)}) async-start(), calls=%async_computation.24 | async-start | bytes 5971968
  1731.3 2.6 copy-start.53
  1731.3 2.7 copy-start.34
  1731.3 2.8 copy-start.32
  1731.3 2.9 copy-start.33
  1731.3 2.9 copy-start.37
  1731.3 45.8 %copy-start.22 = (bf16[1,1152]{1,0:T(2,128)(2,1)S(1)}, bf16[1,1152]{1,0:T(2,128)(2,1)}, u32[]{:S(2)}) copy-start(bf16[1,1152]{1,0:T(2,128)(2,1)} %param.15) | copy-start | bytes 6916
  1731.3 45.8 %copy-start.24 = (f32[1,1152]{1,0:T(1,128)S(1)}, f32[1,1152]{1,0:T(1,128)}, u32[]{:S(2)}) copy-start(f32[1,1152]{1,0:T(1,128)} %copy-done.23) | copy-start | bytes 13828
  (13 other events, 11.1 us)
Sparse Core Ops, SparseCore 0:
  9.6 276.1 all-gather.6
  287.3 140.9 all-gather.8
  429.8 53.5 all-gather.10
  484.9 184.8 all-gather.12
  671.1 184.2 all-gather.14
  897.7 136.2 reduce-scatter.22
  1036.5 180.6 reduce-scatter.26
  1219.6 268.4 reduce-scatter.20
  1490.5 53.2 reduce-scatter.24
  1546.1 179.7 reduce-scatter.28
  1729.3 58.3 reduce-scatter.32
  1791.5 65.4 reduce-scatter.36
  1860.5 82.1 reduce-scatter.30
  1946.5 39.4 reduce-scatter.34
  1989.8 56.9 reduce-scatter.38
where the time goes:
time: 2060 us; the launch traced here: 2050 us
  waiting for transfers between devices  1760 us (85%)
  matrix products  115 us (6%)
  blocking collectives  81.5 us (4%)
  local copies, waits for them, and re-layouts  52.8 us (3%)
  other arithmetic  22.1 us (1%)
    reduce_scatter x1, waiting for transfers between devices, body(): lax.psum_scatter(grad_w_ada.astype(jnp.bfloat16), 'fsdp', scatter_dimensi...  265 us
    unnamed x20, waiting for transfers between devices  255 us
    all_gather x1, waiting for transfers between devices, body(): lax.all_gather(w_ada, 'fsdp', axis=0, tiled=True)  228 us
    all_gather x1, waiting for transfers between devices, body(): lax.all_gather(w_up, 'fsdp', axis=0, tiled=True)  180 us
    reduce_scatter x1, waiting for transfers between devices, body(): lax.psum_scatter(grad_w_down.astype(jnp.bfloat16), 'fsdp', scatter_dimens...  179 us
    reduce_scatter x1, waiting for transfers between devices, body(): lax.psum_scatter(grad_w_up.astype(jnp.bfloat16), 'fsdp', scatter_dimensio...  179 us
    all_gather x1, waiting for transfers between devices, body(): lax.all_gather(w_down, 'fsdp', axis=0, tiled=True)  176 us
    all_gather x1, waiting for transfers between devices, body(): lax.all_gather(w_qkv, 'fsdp', axis=0, tiled=True)  134 us
  transfers between devices with their start and end apart: 15, of which 15 were waited for; matrix products, arithmetic and copies ran while one was open for 7% of the time, Pallas kernels for 0%

commit v1 on v0

--- a/solution.py
+++ b/solution.py
@@ -8,6 +8,27 @@
 epsilon = 1e-06
 masked_value = -1e30
 gelu_root = math.sqrt(2.0 / math.pi)
+
+
+def gather_around(shard, axis, dim):
+    count, mine, rows = (lax.axis_size(axis), lax.axis_index(axis), shard.shape[dim])
+    forward = [(i, (i + 1) % count) for i in range(count)]
+    left = [(i, (i - 1) % count) for i in range(count)]
+    result = jnp.zeros((*shard.shape[:dim], count * rows, *shard.shape[dim + 1 :]), shard.dtype)
+    result = lax.dynamic_update_slice_in_dim(result, shard, mine * rows, axis=dim)
+    from_left = from_right = shard
+    half = count // 2
+    for step in range(1, half + 1):
+        from_left = lax.ppermute(from_left, axis, forward)
+        result = lax.dynamic_update_slice_in_dim(
+            result, from_left, (mine - step) % count * rows, axis=dim
+        )
+        if step < count - half:
+            from_right = lax.ppermute(from_right, axis, left)
+            result = lax.dynamic_update_slice_in_dim(
+                result, from_right, (mine + step) % count * rows, axis=dim
+            )
+    return result
 
 
 def layer_norm(values_in):
@@ -118,7 +139,7 @@
 ):
     weights_full = (
         lax.all_gather(w_ada, "fsdp", axis=0, tiled=True),
-        lax.all_gather(w_qkv, "fsdp", axis=0, tiled=True),
+        gather_around(w_qkv, "fsdp", 0),
         lax.all_gather(w_out, "fsdp", axis=0, tiled=True),
         lax.all_gather(w_up, "fsdp", axis=0, tiled=True),
         lax.all_gather(w_down, "fsdp", axis=0, tiled=True),

time: 2060 us -> 2170 us (1.053)
  blocking collectives: 81.5 us -> 372 us
  waiting for transfers between devices: 1760 us -> 1520 us
  matrix products: 115 us -> 137 us
    all_gather x1, waiting for transfers between devices: 228 us -> 26 us  [body(): lax.all_gather(w_ada, 'fsdp', axis=0, tiled=True)]
    all_gather x1, blocking collectives: 17 us -> 176 us  [body(): lax.all_gather(b_up, 'fsdp', axis=0, tiled=True)]
    unnamed x2, blocking collectives: 41 us -> 173 us
    unnamed x20, waiting for transfers between devices: 255 us -> 234 us
    dot_general x4 -> x7, matrix products: 30.9 us -> 52.2 us  [apply_rows(): jnp.einsum('isd,de->ise', left, right, preferred_element_type=jnp.float32)]
    unnamed x147 -> x195, local copies, waits for them, and re-layouts: 45.7 us -> 51.3 us
  transfers between devices with their start and end apart: 15 -> 18, of which waited for: 15 -> 14; matrix products, arithmetic and copies ran while one was open for 7% -> 9% of each run, Pallas kernels for 0% -> 0%
where the time goes in v1:
time: 2170 us
  waiting for transfers between devices  1520 us (70%)
  blocking collectives  372 us (17%)
  matrix products  137 us (6%)
  local copies, waits for them, and re-layouts  72.6 us (3%)
  other arithmetic  27.3 us (1%)
    reduce_scatter x1, waiting for transfers between devices, body(): lax.psum_scatter(grad_w_ada.astype(jnp.bfloat16), 'fsdp', scatter_dimensi...  265 us
    unnamed x20, waiting for transfers between devices  234 us
    all_gather x1, waiting for transfers between devices, body(): lax.all_gather(w_up, 'fsdp', axis=0, tiled=True)  182 us
    reduce_scatter x1, waiting for transfers between devices, body(): lax.psum_scatter(grad_w_down.astype(jnp.bfloat16), 'fsdp', scatter_dimens...  179 us
    reduce_scatter x1, waiting for transfers between devices, body(): lax.psum_scatter(grad_w_up.astype(jnp.bfloat16), 'fsdp', scatter_dimensio...  179 us
    all_gather x1, waiting for transfers between devices, body(): lax.all_gather(w_down, 'fsdp', axis=0, tiled=True)  177 us
    all_gather x1, blocking collectives, body(): lax.all_gather(b_up, 'fsdp', axis=0, tiled=True)  176 us
    unnamed x2, blocking collectives  173 us
  transfers between devices with their start and end apart: 18, of which 14 were waited for; matrix products, arithmetic and copies ran while one was open for 9% of the time, Pallas kernels for 0%

profile of v1, /device:TPU:0, one launch (start us, length us, event | category | flops | bytes accessed | tf_op | source)
XLA Modules:
  0.0 2167.0 jit_solution(12176518160756075870)
XLA Ops:
  11.0 3.0 collective-permute-start
  14.0 2.0 collective-permute-start.1
  17.9 175.6 %all-gather = bf16[4,1,1152]{2,1,0:T(2,128)(2,1)S(1)} all-gather(bf16[1,1,1152]{2,1,0:T(2,128)(2,1)S(1)} %reshape.580), channel_id=1, replica_groups=mesh['dp'=8,'fsdp'=4] {'fsdp'}, dimensions={0}, use_global_device_ids=true | all-gather | bytes 11520 | tf_op jit(solution)/shard_map/all_gather | solution.py:149
  194.7 7.8 collective-permute-start.2
  206.7 153.7 %all-reduce.11 = (bf16[2304]{0:T(1024)(128)(2,1)S(1)}, bf16[6912]{0:T(1024)(128)(2,1)S(1)}, bf16[1152]{0:T(1024)(128)(2,1)S(1)}, bf16[1152]{0:T(1024)(128)(2,1)}) all-reduce(bf16[2304]{0:T(1024)(128)(2,1)S(1)} %dynamic-update-slice.1, bf16[6912]{0:T(1024)(128)(2,1)S(1)} %dynamic-update-slice, ...), channel_id=1, replica_groups=mesh['dp'=8,'fsdp'=4] {'fsdp'}, use_global_device_ids=true, to_apply=%add.1 | all-reduce | flops 11520 | bytes 46080
  362.2 3.7 broadcast_in_dim.26
  365.9 1.5 constant_dynamic-update-slice_fusion.3
  367.4 3.0 constant_dynamic-update-slice_fusion.2
  370.4 3.0 constant_dynamic-update-slice_fusion.1
  373.4 3.1 constant_dynamic-update-slice_fusion
  376.4 26.0 %all-gather.7.cloned.1.call-done = bf16[1152,6912]{1,0:T(8,128)(2,1)} async-done(((bf16[288,6912]{1,0:T(8,128)(2,1)}), bf16[1152,6912]{1,0:T(8,128)(2,1)}) %all-gather.7.cloned.1.call-update) | async-done | bytes 15925264 | tf_op jit(solution)/shard_map/all_gather | solution.py:141
  402.5 7.7 convolution_reduce_fusion
  410.9 6.8 convolution_bitcast_fusion.1
  417.7 1.8 copy-done.13
  419.6 126.3 %all-gather.15.cloned.1.call-done = bf16[1152,3456]{1,0:T(8,128)(2,1)} async-done(((bf16[288,3456]{1,0:T(8,128)(2,1)}), bf16[1152,3456]{1,0:T(8,128)(2,1)}) %all-gather.15.cloned.1.call-update) | async-done | bytes 7962640 | tf_op jit(solution)/shard_map/all_gather | solution.py:169
  546.0 6.1 convolution_bitcast_fusion
  556.4 2.4 fusion.11
  561.5 2.1 copy-done
  564.7 36.5 %all-gather.9.cloned.1.call-done = bf16[1152,1152]{1,0:T(8,128)(2,1)} async-done(((bf16[288,1152]{1,0:T(8,128)(2,1)}), bf16[1152,1152]{1,0:T(8,128)(2,1)}) %all-gather.9.cloned.1.call-update) | async-done | bytes 2654224 | tf_op jit(solution)/shard_map/all_gather | solution.py:143
  601.2 3.9 fusion.99
  605.4 182.1 %all-gather.11.cloned.1.call-done = bf16[1152,4608]{1,0:T(8,128)(2,1)} async-done(((bf16[288,4608]{1,0:T(8,128)(2,1)}), bf16[1152,4608]{1,0:T(8,128)(2,1)}) %all-gather.11.cloned.1.call-update) | async-done | bytes 10616848 | tf_op jit(solution)/shard_map/all_gather | solution.py:144
  787.5 9.1 convolution_add_fusion
  796.6 176.5 %all-gather.13.cloned.1.call-done = bf16[4608,1152]{1,0:T(8,128)(2,1)} async-done(((bf16[1152,1152]{1,0:T(8,128)(2,1)}), bf16[4608,1152]{1,0:T(8,128)(2,1)}) %all-gather.13.cloned.1.call-update) | async-done | bytes 10616848 | tf_op jit(solution)/shard_map/all_gather | solution.py:145
  973.2 10.5 fusion.104
  983.7 3.9 fusion.47
  991.0 1.9 convolution_convert_fusion.4
  992.8 2.1 copy.67
  994.9 4.3 bitcast_reduce_fusion
  999.3 1.5 multiply_reduce_fusion
  1005.0 5.9 convolution_convert_fusion.2
  1011.6 8.7 convolution_convert_fusion.1
  1023.8 7.0 fusion.42
  1031.4 1.5 dynamic-update-slice.4
  1034.2 1.9 fusion.40
  1036.1 1.5 dynamic-update-slice.5
  1038.2 3.4 fusion.48
  1041.6 1.5 dynamic-update-slice.6
  1043.1 1.4 dynamic-update-slice.7
  1045.9 9.0 fusion.37
  1055.2 5.9 multiply_convert_fusion
  1062.3 2.4 convolution_convert_fusion.3
  1065.5 10.8 convolution_convert_fusion
  1076.3 71.0 %reduce-scatter.23.cloned.1.call-done = bf16[288,3456]{1,0:T(8,128)(2,1)} async-done(((bf16[1152,3456]{1,0:T(8,128)(2,1)}), bf16[288,3456]{1,0:T(8,128)(2,1)}) %reduce-scatter.23.cloned.1.call-update) | async-done | bytes 1990672 | tf_op jit(solution)/shard_map/reduce_scatter | solution.py:274
  1147.4 4.5 copy.80
  1152.0 178.6 %reduce-scatter.27.cloned.1.call-done = bf16[288,4608]{1,0:T(8,128)(2,1)} async-done(((bf16[1152,4608]{1,0:T(8,128)(2,1)}), bf16[288,4608]{1,0:T(8,128)(2,1)}) %reduce-scatter.27.cloned.1.call-update) | async-done | bytes 2654224 | tf_op jit(solution)/shard_map/reduce_scatter | solution.py:280
  1330.6 5.5 copy.84
  1336.1 265.3 %reduce-scatter.21.cloned.1.call-done = bf16[288,6912]{1,0:T(8,128)(2,1)} async-done(((bf16[1152,6912]{1,0:T(8,128)(2,1)}), bf16[288,6912]{1,0:T(8,128)(2,1)}) %reduce-scatter.21.cloned.1.call-update) | async-done | bytes 3981328 | tf_op jit(solution)/shard_map/reduce_scatter | solution.py:271
  1601.5 7.7 copy.78
  1609.2 47.9 %reduce-scatter.25.cloned.1.call-done = bf16[288,1152]{1,0:T(8,128)(2,1)} async-done(((bf16[1152,1152]{1,0:T(8,128)(2,1)}), bf16[288,1152]{1,0:T(8,128)(2,1)}) %reduce-scatter.25.cloned.1.call-update) | async-done | bytes 663568 | tf_op jit(solution)/shard_map/reduce_scatter | solution.py:277
  1657.1 2.7 copy.82
  1659.8 179.4 %reduce-scatter.29.cloned.1.call-done = bf16[1152,1152]{1,0:T(8,128)(2,1)} async-done(((bf16[4608,1152]{1,0:T(8,128)(2,1)}), bf16[1152,1152]{1,0:T(8,128)(2,1)}) %reduce-scatter.29.cloned.1.call-update) | async-done | bytes 2654224 | tf_op jit(solution)/shard_map/reduce_scatter | solution.py:283
  1839.3 5.4 copy.86
  1847.8 19.2 all-reduce.10
  1867.3 23.7 %all-reduce.9 = (f32[1728]{0:T(1024)}, f32[576]{0:T(1024)}, f32[288]{0:T(512)}, f32[1152]{0:T(1024)}, f32[288]{0:T(512)}) all-reduce(f32[1728]{0:T(1024)S(1)} %dynamic-slice_convert_fusion.1, f32[576]{0:T(1024)S(1)} %dynamic-slice_convert_fusion.2, f32[288]{0:T(512)S(1)} %get-tuple-element.116, ...), channel_id=1, replica_groups=mesh['dp'=8,'fsdp'=4] {'dp'}, use_global_device_ids=true, to_apply=%region_30.31 | all-reduce | flops 4032 | bytes 32256 | tf_op jit(solution)/shard_map/psum | solution.py:309
  1891.1 3.4 fusion.36
  1896.1 10.5 fusion.72
  1906.6 16.1 fusion.21
  1922.7 2.1 copy.81
  1924.9 45.5 %reduce-scatter.37.cloned.1.call-done = f32[576,288]{1,0:T(8,128)} async-done(((f32[4608,288]{1,0:T(8,128)}), f32[576,288]{1,0:T(8,128)}) %reduce-scatter.37.cloned.1.call-update) | async-done | bytes 663568
  1970.4 2.3 copy.85
  1972.7 83.4 %reduce-scatter.31.cloned.1.call-done = f32[864,288]{1,0:T(8,128)} async-done(((f32[6912,288]{1,0:T(8,128)}), f32[864,288]{1,0:T(8,128)}) %reduce-scatter.31.cloned.1.call-update) | async-done | bytes 995344
  2056.1 2.7 copy.79
  2058.8 40.5 %reduce-scatter.35.cloned.1.call-done = f32[144,288]{1,0:T(8,128)} async-done(((f32[1152,288]{1,0:T(8,128)}), f32[144,288]{1,0:T(8,128)}) %reduce-scatter.35.cloned.1.call-update) | async-done | bytes 165904
  2099.4 60.8 %reduce-scatter.39.cloned.1.call-done = f32[144,1152]{1,0:T(8,128)} async-done(((f32[1152,1152]{1,0:T(8,128)}), f32[144,1152]{1,0:T(8,128)}) %reduce-scatter.39.cloned.1.call-update) | async-done | bytes 663568
  (274 shorter events, 39.1 us)
Async XLA Ops:
  7.2 395.3 %all-gather.7.cloned.1.call-start = ((), (), s32[]{:S(2)}) async-start(), calls=%async_computation.10 | async-start | bytes 19906560 | tf_op jit(solution)/shard_map/all_gather | solution.py:141
  7.9 538.1 %all-gather.15.cloned.1.call-start = ((), (), s32[]{:S(2)}) async-start(), calls=%async_computation.14 | async-start | bytes 9953280 | tf_op jit(solution)/shard_map/all_gather | solution.py:169
  8.7 592.5 %all-gather.9.cloned.1.call-start = ((), (), s32[]{:S(2)}) async-start(), calls=%async_computation.11 | async-start | bytes 3317760 | tf_op jit(solution)/shard_map/all_gather | solution.py:143
  9.4 6.6 copy-start.76
  9.4 6.6 copy-start.81
  9.4 184.2 %copy-start.3 = (bf16[1,256,1152]{2,1,0:T(8,128)(2,1)S(1)}, bf16[1,256,1152]{2,1,0:T(8,128)(2,1)}, u32[]{:S(2)}) copy-start(bf16[1,256,1152]{2,1,0:T(8,128)(2,1)} %param.14) | copy-start | bytes 1769476
  9.4 778.0 %all-gather.11.cloned.1.call-start = ((), (), s32[]{:S(2)}) async-start(), calls=%async_computation.12 | async-start | bytes 13271040 | tf_op jit(solution)/shard_map/all_gather | solution.py:144
  10.0 193.0 %copy-start.79 = (u32[32]{0:T(128)S(1)}, u32[32]{0:T(128)}, u32[]{:S(2)}) copy-start(u32[32]{0:T(128)} %constant.85) | copy-start | bytes 388
  10.0 195.6 %copy-start.82 = (bf16[288]{0:T(512)(128)(2,1)S(1)}, bf16[288]{0:T(512)(128)(2,1)}, u32[]{:S(2)}) copy-start(bf16[288]{0:T(512)(128)(2,1)} %param.24) | copy-start | bytes 1732
  10.0 195.8 %copy-start.83 = (bf16[288]{0:T(512)(128)(2,1)S(1)}, bf16[288]{0:T(512)(128)(2,1)}, u32[]{:S(2)}) copy-start(bf16[288]{0:T(512)(128)(2,1)} %param.26) | copy-start | bytes 1732
  10.0 196.1 %copy-start.80 = (bf16[576]{0:T(1024)(128)(2,1)S(1)}, bf16[576]{0:T(1024)(128)(2,1)}, u32[]{:S(2)}) copy-start(bf16[576]{0:T(1024)(128)(2,1)} %param.23) | copy-start | bytes 3460
  10.1 196.3 %copy-start.77 = (bf16[1728]{0:T(1024)(128)(2,1)S(1)}, bf16[1728]{0:T(1024)(128)(2,1)}, u32[]{:S(2)}) copy-start(bf16[1728]{0:T(1024)(128)(2,1)} %param.22) | copy-start | bytes 10372
  10.1 351.5 %copy-start.40 = (bf16[1,1152]{1,0:T(2,128)(2,1)S(1)}, bf16[1,1152]{1,0:T(2,128)(2,1)}, u32[]{:S(2)}) copy-start(bf16[1,1152]{1,0:T(2,128)(2,1)} %param.15) | copy-start | bytes 6916
  10.1 963.1 %all-gather.13.cloned.1.call-start = ((), (), s32[]{:S(2)}) async-start(), calls=%async_computation.13 | async-start | bytes 13271040 | tf_op jit(solution)/shard_map/all_gather | solution.py:145
  10.7 1136.7 %reduce-scatter.23.cloned.1.call-start = ((), (), s32[]{:S(2)}) async-start(), calls=%async_computation.16 | async-start | bytes 9953280 | tf_op jit(solution)/shard_map/reduce_scatter | solution.py:274
  11.0 183.7 %collective-permute-start = (bf16[288,3456]{1,0:T(8,128)(2,1)S(1)}, bf16[288,3456]{1,0:T(8,128)(2,1)}, u32[]{:S(2)}, u32[]{:S(2)}) collective-permute-start(bf16[288,3456]{1,0:T(8,128)(2,1)S(1)} %copy-done.4), channel_id=1, source_target_pairs={{0,1},{1,2},{2,3},{3,0},{4,5},{5,6},{6,7},{7,4},{8,9},{9,10},{10,1... | collective-permute-start | bytes 5971976 | tf_op jit(solution)/shard_map/ppermute | solution.py:22
  14.0 356.4 %collective-permute-start.1 = (bf16[288,3456]{1,0:T(8,128)(2,1)S(1)}, bf16[288,3456]{1,0:T(8,128)(2,1)}, u32[]{:S(2)}, u32[]{:S(2)}) collective-permute-start(bf16[288,3456]{1,0:T(8,128)(2,1)S(1)} %copy-done.4), channel_id=1, source_target_pairs={{0,3},{1,0},{2,1},{3,2},{4,7},{5,4},{6,5},{7,6},{8,11},{9,8},{10,9... | collective-permute-start | bytes 5971976 | tf_op jit(solution)/shard_map/ppermute | solution.py:27
  193.8 352.2 %copy-start.53 = (f32[256]{0:T(256)}, f32[256]{0:T(256)S(1)}, u32[]{:S(2)}) copy-start(f32[256]{0:T(256)S(1)} %broadcast_multiply_fusion.2) | copy-start | bytes 3076
  194.6 11.7 copy-start.65
  194.7 351.3 %copy-start.55 = (f32[256]{0:T(256)}, f32[256]{0:T(256)S(1)}, u32[]{:S(2)}) copy-start(f32[256]{0:T(256)S(1)} %fusion.77) | copy-start | bytes 3076
  194.7 178.7 %collective-permute-start.2 = (bf16[288,3456]{1,0:T(8,128)(2,1)}, bf16[288,3456]{1,0:T(8,128)(2,1)}, u32[]{:S(2)}, u32[]{:S(2)}) collective-permute-start(bf16[288,3456]{1,0:T(8,128)(2,1)} %collective-permute-done), channel_id=1, source_target_pairs={{0,1},{1,2},{2,3},{3,0},{4,5},{5,6},{6,7},{7,4},{8,9},{9,10},{10,1... | collective-permute-start | bytes 5971976 | tf_op jit(solution)/shard_map/ppermute | solution.py:22
  362.2 40.3 %copy-start.42 = (f32[1,1152]{1,0:T(1,128)}, f32[1,1152]{1,0:T(1,128)S(1)}, u32[]{:S(2)}) copy-start(f32[1,1152]{1,0:T(1,128)S(1)} %get-tuple-element.79) | copy-start | bytes 13828
  410.9 135.1 %copy-start.35 = (f32[1152]{0:T(1024)}, f32[1152]{0:T(1024)S(1)}, u32[]{:S(2)}) copy-start(f32[1152]{0:T(1024)S(1)} %get-tuple-element.60) | copy-start | bytes 13828
  410.9 135.1 %copy-start.66 = (f32[1152]{0:T(1024)}, f32[1152]{0:T(1024)S(1)}, u32[]{:S(2)}) copy-start(f32[1152]{0:T(1024)S(1)} %get-tuple-element.59) | copy-start | bytes 13828
  546.0 6.2 copy-start.14
  555.8 5.6 copy-start.16
  556.1 4.6 copy-start.5
  564.7 40.4 %copy-start.9 = (bf16[16,72,256]{2,1,0:T(8,128)(2,1)}, bf16[16,72,256]{2,1,0:T(8,128)(2,1)S(1)}, u32[]{:S(2)}) copy-start(bf16[16,72,256]{2,1,0:T(8,128)(2,1)S(1)} %convolution_convert_fusion.6) | copy-start | bytes 1769476
  601.2 186.3 %copy-start.28 = (f32[1152]{0:T(1024)S(1)}, f32[1152]{0:T(1024)}, u32[]{:S(2)}) copy-start(f32[1152]{0:T(1024)} %get-tuple-element.58) | copy-start | bytes 13828
  601.2 186.3 %copy-start.37 = (f32[1152]{0:T(1024)S(1)}, f32[1152]{0:T(1024)}, u32[]{:S(2)}) copy-start(f32[1152]{0:T(1024)} %get-tuple-element.57) | copy-start | bytes 13828
  601.2 186.3 %copy-start.51 = (f32[4608]{0:T(1024)S(1)}, f32[4608]{0:T(1024)}, u32[]{:S(2)}) copy-start(f32[4608]{0:T(1024)} %reshape.582) | copy-start | bytes 55300
  605.1 378.6 %copy-start.49 = (f32[256]{0:T(256)}, f32[256]{0:T(256)S(1)}, u32[]{:S(2)}) copy-start(f32[256]{0:T(256)S(1)} %broadcast_multiply_fusion) | copy-start | bytes 3076
  605.4 378.3 %copy-start.60 = (f32[256]{0:T(256)}, f32[256]{0:T(256)S(1)}, u32[]{:S(2)}) copy-start(f32[256]{0:T(256)S(1)} %fusion.78) | copy-start | bytes 3076
  787.5 185.7 %copy-start.19 = (bf16[1,256,1152]{2,1,0:T(8,128)(2,1)S(1)}, bf16[1,256,1152]{2,1,0:T(8,128)(2,1)}, u32[]{:S(2)}) copy-start(bf16[1,256,1152]{2,1,0:T(8,128)(2,1)} %param.27) | copy-start | bytes 1769476
  787.5 185.7 %copy-start.44 = (f32[1152]{0:T(1024)S(1)}, f32[1152]{0:T(1024)}, u32[]{:S(2)}) copy-start(f32[1152]{0:T(1024)} %get-tuple-element.56) | copy-start | bytes 13828
  787.5 185.7 %copy-start.73 = (f32[256]{0:T(256)S(1)}, f32[256]{0:T(256)}, u32[]{:S(2)}) copy-start(f32[256]{0:T(256)} %fusion.87) | copy-start | bytes 3076
  973.2 10.5 copy-start.84
  983.7 3.9 copy-start.24
  983.7 3.9 copy-start.29
  994.9 4.3 copy-start.1
  994.9 4.3 copy-start.17
  994.9 4.3 copy-start.18
  994.9 4.3 copy-start.71
  999.3 4.9 copy-start.85
  1010.9 319.6 %reduce-scatter.27.cloned.1.call-start = ((), (), s32[]{:S(2)}) async-start(), calls=%async_computation.18 | async-start | bytes 13271040 | tf_op jit(solution)/shard_map/reduce_scatter | solution.py:280
  1020.4 581.1 %reduce-scatter.21.cloned.1.call-start = ((), (), s32[]{:S(2)}) async-start(), calls=%async_computation.15 | async-start | bytes 19906560 | tf_op jit(solution)/shard_map/reduce_scatter | solution.py:271
  1030.8 7.4 copy-start.21
  1045.9 9.0 copy-start.32
  1045.9 9.2 copy-start.48
  1061.1 596.0 %reduce-scatter.25.cloned.1.call-start = ((), (), s32[]{:S(2)}) async-start(), calls=%async_computation.17 | async-start | bytes 3317760 | tf_op jit(solution)/shard_map/reduce_scatter | solution.py:277
  1064.8 774.5 %reduce-scatter.29.cloned.1.call-start = ((), (), s32[]{:S(2)}) async-start(), calls=%async_computation.19 | async-start | bytes 13271040 | tf_op jit(solution)/shard_map/reduce_scatter | solution.py:283
  1076.3 846.5 %reduce-scatter.33.cloned.1.call-start = ((), (), s32[]{:S(2)}) async-start(), calls=%async_computation.21 | async-start | bytes 5971968
  1151.9 818.5 %reduce-scatter.37.cloned.1.call-start = ((), (), s32[]{:S(2)}) async-start(), calls=%async_computation.23 | async-start | bytes 7962624
  1336.1 720.0 %reduce-scatter.31.cloned.1.call-start = ((), (), s32[]{:S(2)}) async-start(), calls=%async_computation.20 | async-start | bytes 11943936
  1609.1 490.2 %reduce-scatter.35.cloned.1.call-start = ((), (), s32[]{:S(2)}) async-start(), calls=%async_computation.22 | async-start | bytes 1990656
  1659.8 500.4 %reduce-scatter.39.cloned.1.call-start = ((), (), s32[]{:S(2)}) async-start(), calls=%async_computation.24 | async-start | bytes 5971968
  1844.7 46.4 %copy-start.72 = (pred[256]{0:T(512)(128)(4,1)S(1)}, pred[256]{0:T(512)(128)(4,1)}, u32[]{:S(2)}) copy-start(pred[256]{0:T(512)(128)(4,1)} %iota_compare_fusion) | copy-start | bytes 772
  1891.0 3.5 copy-start.12
  1891.1 3.5 copy-start.34
  1891.1 3.5 copy-start.47
  1896.0 10.6 copy-start.31
  1896.1 10.6 copy-start.39
  1896.1 10.6 copy-start.52
  1896.1 10.6 copy-start.68
  (40 other events, 72.0 us)
Sparse Core Ops, SparseCore 0:
  9.6 392.8 all-gather.6
  404.1 141.8 all-gather.14
  547.6 53.5 all-gather.8
  602.6 184.8 all-gather.10
  788.9 184.2 all-gather.12
  1011.1 136.2 reduce-scatter.22
  1149.8 180.6 reduce-scatter.26
  1333.0 268.4 reduce-scatter.20
  1603.9 53.2 reduce-scatter.24
  1659.4 179.8 reduce-scatter.28
  1842.7 58.3 reduce-scatter.32
  1904.9 65.4 reduce-scatter.36
  1973.9 82.1 reduce-scatter.30
  2059.9 39.4 reduce-scatter.34
  2103.2 56.9 reduce-scatter.38
